TPU v7x, 512 devices: a whole 4x8x8 slice. The times are simulated.
512 devices in a mesh: ta: 8 (over y), gz: 8 (over x, core), xy: 8 (over z).
Axes of the slice: x: 4, y: 8, z: 8, core: 2. Of those that a mesh axis runs over, the one named last changes fastest.
Arguments:
- right_side: float32 [8, 8, 8, 2, 32, 128], P('ta', 'gz', 'xy'), may hold values from -40 to 40
- stencil: float32 [8, 8, 8, 2, 9, 128, 128], P('ta', 'gz', 'xy'), may hold values from -0.5 to 1.5, as said below
- restrict: float32 [8, 8, 8, 2, 32, 128], P('ta', 'gz', 'xy'), may hold values from -0.5 to 0.5
- aggregate: int32 [8, 8, 8, 2], P('ta', 'gz', 'xy'), may hold values from 0 to 63, as said below
- coarsest_inverse: float32 [2048, 2048], P('xy'), may hold values from -0.125 to 0.125
Outputs:
- solution: float32 [8, 8, 8, 2, 32, 128], P('ta', 'gz', 'xy')
- residual: float32 [8, 8, 8, 2, 32, 128], P('ta', 'gz', 'xy')
Inputs may be any that keep to these rules, and one draw needn't show every extreme that they name: `aggregate`: sites are grouped into 2 x 2 x 2 x 2 blocks aligned at even coordinates; each block forms one coarsest site, and the coarsest sites are numbered in an order drawn from the seed. `stencil`: each self block is close to the identity; the other blocks are small and full.
All inputs are finite; a program needn't handle non-finite values.
Results may differ from a plain program's by a relative error of at most 0.0001.
Values sent between devices are 32-bit elements; how exact they have to be, the bound alone decides.
No kernel may reach another device: no remote copies, remote signals or barrier semaphores. Data moves between devices by JAX's collectives and lax.ppermute only.
A program may use at most 64 MiB of HBM per device.

v0:
```python
import jax
import jax.numpy as jnp
from jax import lax
from jax.sharding import PartitionSpec as P


def extended(cells, sides, width):
    for axis, dim in sides:
        count = lax.axis_size(axis)
        head = lax.slice_in_dim(cells, 0, width, axis=dim)
        tail = lax.slice_in_dim(cells, cells.shape[dim] - width, cells.shape[dim], axis=dim)
        cells = jnp.concatenate(
            [
                lax.ppermute(tail, axis, [(i, (i + 1) % count) for i in range(count)]),
                cells,
                lax.ppermute(head, axis, [((i + 1) % count, i) for i in range(count)]),
            ],
            axis=dim,
        )
    return cells


def apply_operator(field, stencil):
    padded = extended(field, (("ta", 0), ("gz", 1), ("xy", 2)), 1)
    centre = field[0, 0, 0]
    stacked = jnp.stack(
        [
            centre,
            padded[2, 1, 1],
            padded[0, 1, 1],
            padded[1, 2, 1],
            padded[1, 0, 1],
            padded[1, 1, 2],
            padded[1, 1, 0],
            jnp.roll(centre, -1, 0),
            jnp.roll(centre, 1, 0),
        ],
        axis=1,
    )
    result = jnp.einsum(
        "xkij,xkrj->xri", stencil[0, 0, 0], stacked, precision=lax.Precision.HIGHEST
    )
    return result[None, None, None]


def inner_sum(one_side, other_side):
    return jnp.sum(one_side * other_side, axis=(0, 1, 2, 3, 5))


def body(right_side, stencil, restrict, aggregate, coarsest_inverse):
    image_first = apply_operator(right_side, stencil)
    cross_first, square_first = lax.psum(
        (inner_sum(image_first, right_side), inner_sum(image_first, image_first)),
        ("ta", "gz", "xy"),
    )
    step_first = cross_first / square_first
    resid_mid = right_side - step_first[:, None] * image_first
    image_raw = apply_operator(resid_mid, stencil)
    correlation_sum = lax.psum(inner_sum(image_first, image_raw), ("ta", "gz", "xy"))
    beta = correlation_sum / square_first
    image_second = image_raw - beta[:, None] * image_first
    direction = resid_mid - beta[:, None] * right_side
    cross_second, square_second = lax.psum(
        (inner_sum(image_second, resid_mid), inner_sum(image_second, image_second)),
        ("ta", "gz", "xy"),
    )
    step_second = cross_second / square_second
    solution_gcr = step_first[:, None] * right_side + step_second[:, None] * direction
    residual = resid_mid - step_second[:, None] * image_second
    vectors = restrict[0, 0, 0]
    comps = vectors.shape[1]
    aggregates = coarsest_inverse.shape[1] // comps
    nrhs_count = residual.shape[4]
    restricted = jnp.einsum(
        "xkc,xrc->xrk", vectors, residual[0, 0, 0], precision=lax.Precision.HIGHEST
    )
    labels = aggregate[0, 0, 0]
    onehot = (labels[:, None] == jnp.arange(aggregates, dtype=jnp.int32)[None, :]).astype(
        jnp.float32
    )
    partial_rhs = jnp.einsum("xa,xrk->akr", onehot, restricted, precision=lax.Precision.HIGHEST)
    partial_rhs = partial_rhs.reshape(aggregates * comps, nrhs_count)
    coarse_rhs = lax.psum(partial_rhs, ("ta", "gz", "xy"))
    rows_part = jnp.dot(
        coarsest_inverse,
        coarse_rhs,
        precision=lax.Precision.HIGHEST,
        preferred_element_type=jnp.float32,
    )
    correction = lax.all_gather(rows_part, "xy", axis=0, tiled=True)
    correction = correction.reshape(aggregates, comps, nrhs_count)
    per_site = jnp.einsum("xa,akr->xkr", onehot, correction, precision=lax.Precision.HIGHEST)
    lifted = jnp.einsum("xkc,xkr->xrc", vectors, per_site, precision=lax.Precision.HIGHEST)
    solution = solution_gcr + lifted[None, None, None]
    return (solution, residual)


def solution(mesh):
    return jax.shard_map(
        body,
        mesh=mesh,
        in_specs=(
            P("ta", "gz", "xy", None, None, None),
            P("ta", "gz", "xy", None, None, None, None),
            P("ta", "gz", "xy", None, None, None),
            P("ta", "gz", "xy", None),
            P("xy", None),
        ),
        out_specs=(P("ta", "gz", "xy", None, None, None), P("ta", "gz", "xy", None, None, None)),
        check_vma=False,
    )
```

profile of v0, /device:TPU:26, one launch (start us, length us, event | category | flops | bytes accessed | tf_op | source)
XLA Modules:
  0.0 679.4 jit_solution(10552285033728135520)
XLA Ops:
  7.2 5.0 collective-permute-start.1
  12.2 1.9 collective-permute-start
  16.4 3.0 collective-permute-done
  19.5 1.7 collective-permute-start.2
  21.2 2.3 collective-permute-done.3
  23.5 4.3 collective-permute-start.5
  27.8 8.6 %collective-permute-start.4 = (f32[3,3,1,2,32,128]{5,4,3,2,1,0:T(8,128)S(1)}, f32[3,3,1,2,32,128]{5,4,3,2,1,0:T(8,128)S(1)}, u32[]{:S(2)}, u32[]{:S(2)}) collective-permute-start(f32[3,3,1,2,32,128]{5,4,3,2,1,0:T(8,128)S(1)} %pad_maximum_fusion), channel_id=1, source_target_pairs={{1,0},{2,1},{3,2},{4,3},{5,4},{6,5},{7,6},{0,7},{9,8},{10,9},{11,1... | collective-permute-start | bytes 884744 | tf_op jit(solution)/shard_map/ppermute | solution.py:16
  36.4 6.7 collective-permute-done.4
  44.8 97.5 %all-reduce.1 = (f32[32]{0:T(128)S(1)}, f32[32]{0:T(128)S(1)}) all-reduce(f32[32]{0:T(128)S(1)} %get-tuple-element.14, f32[32]{0:T(128)S(1)} %fusion.13), channel_id=1, replica_groups=mesh['ta'=8,'gz'=8,'xy'=8] {'ta','gz','xy'}, use_global_device_ids=true, to_apply=%region_1.2 | all-reduce | flops 64 | bytes 512 | tf_op jit(solution)/shard_map/psum | solution.py:52
  142.3 4.1 collective-permute-start.7
  146.4 1.9 collective-permute-start.6
  148.3 5.1 collective-permute-done.6
  153.4 1.7 collective-permute-start.8
  155.2 2.3 collective-permute-done.9
  157.5 1.9 collective-permute-start.11
  159.5 5.1 collective-permute-start.10
  164.6 6.2 collective-permute-done.10
  172.3 97.8 %psum.44 = f32[32]{0:T(128)S(1)} all-reduce(f32[32]{0:T(128)S(1)} %get-tuple-element.16), channel_id=1, replica_groups=mesh['ta'=8,'gz'=8,'xy'=8] {'ta','gz','xy'}, use_global_device_ids=true, to_apply=%region_5.6 | all-reduce | flops 32 | bytes 256 | tf_op jit(solution)/shard_map/psum | solution.py:59
  270.5 94.5 %all-reduce = (f32[32]{0:T(128)S(1)}, f32[32]{0:T(128)S(1)}) all-reduce(f32[32]{0:T(128)S(1)} %fusion.11, f32[32]{0:T(128)S(1)} %get-tuple-element.6), channel_id=1, replica_groups=mesh['ta'=8,'gz'=8,'xy'=8] {'ta','gz','xy'}, use_global_device_ids=true, to_apply=%region_7.8 | all-reduce | flops 64 | bytes 512 | tf_op jit(solution)/shard_map/psum | solution.py:63
  365.2 1.4 convolution_bitcast_fusion
  369.3 267.9 %all-reduce.4.cloned.1.call-done = f32[2048,32]{0,1:T(8,128)} async-done(((f32[2048,32]{0,1:T(8,128)}), f32[2048,32]{0,1:T(8,128)}) %all-reduce.4.cloned.1.call-update) | async-done | bytes 262160 | tf_op jit(solution)/shard_map/psum | solution.py:83
  637.2 2.9 convolution_bitcast_fusion.2
  640.1 26.9 %all_gather.3 = f32[2048,32]{0,1:T(8,128)} all-gather(f32[256,32]{0,1:T(8,128)S(1)} %convolution_bitcast_fusion.2), channel_id=1, replica_groups=mesh['ta'=8,'gz'=8,'xy'=8] {'xy'}, dimensions={0}, use_global_device_ids=true | all-gather | bytes 294912 | tf_op jit(solution)/shard_map/all_gather | solution.py:90
  669.5 2.2 fusion.17
  (63 shorter events, 12.1 us)
Async XLA Ops:
  7.2 630.0 %copy-start = (f32[256,2048]{1,0:T(8,128)S(1)}, f32[256,2048]{1,0:T(8,128)}, u32[]{:S(2)}) copy-start(f32[256,2048]{1,0:T(8,128)} %param.9) | copy-start | bytes 6291460
  7.2 36.0 %copy-start.2 = (f32[1,1,1,2,32,128]{5,4,3,2,1,0:T(8,128)S(1)}, f32[1,1,1,2,32,128]{5,4,3,2,1,0:T(8,128)}, u32[]{:S(2)}) copy-start(f32[1,1,1,2,32,128]{5,4,3,2,1,0:T(8,128)} %param.5) | copy-start | bytes 98308
  7.2 36.0 %copy-start.1 = (f32[1,1,1,2,9,128,128]{6,5,4,3,2,1,0:T(8,128)S(1)}, f32[1,1,1,2,9,128,128]{6,5,4,3,2,1,0:T(8,128)}, u32[]{:S(2)}) copy-start(f32[1,1,1,2,9,128,128]{6,5,4,3,2,1,0:T(8,128)} %param.6) | copy-start | bytes 3538948
  7.2 630.0 %all-reduce.4.cloned.1.call-start = ((), (), s32[]{:S(2)}) async-start(), calls=%async_computation | async-start | bytes 524288 | tf_op jit(solution)/shard_map/psum | solution.py:83
  7.2 8.4 %collective-permute-start.1 = (f32[1,1,1,2,32,128]{5,4,3,2,1,0:T(8,128)}, f32[1,1,1,2,32,128]{5,4,3,2,1,0:T(8,128)S(1)}, u32[]{:S(2)}, u32[]{:S(2)}) collective-permute-start(f32[1,1,1,2,32,128]{5,4,3,2,1,0:T(8,128)} %param.5), channel_id=1, source_target_pairs={{0,64},{64,128},{128,192},{192,256},{256,320},{320,384},{384,448},... | collective-permute-start | bytes 98312 | tf_op jit(solution)/shard_map/ppermute | solution.py:14
  12.2 7.2 %collective-permute-start = (f32[1,1,1,2,32,128]{5,4,3,2,1,0:T(8,128)}, f32[1,1,1,2,32,128]{5,4,3,2,1,0:T(8,128)S(1)}, u32[]{:S(2)}, u32[]{:S(2)}) collective-permute-start(f32[1,1,1,2,32,128]{5,4,3,2,1,0:T(8,128)} %param.5), channel_id=1, source_target_pairs={{64,0},{128,64},{192,128},{256,192},{320,256},{384,320},{448,384},... | collective-permute-start | bytes 98312 | tf_op jit(solution)/shard_map/ppermute | solution.py:16
  19.5 4.0 collective-permute-start.3
  19.5 4.0 collective-permute-start.2
  23.5 19.6 %collective-permute-start.5 = (f32[3,3,1,2,32,128]{5,4,3,2,1,0:T(8,128)S(1)}, f32[3,3,1,2,32,128]{5,4,3,2,1,0:T(8,128)S(1)}, u32[]{:S(2)}, u32[]{:S(2)}) collective-permute-start(f32[3,3,1,2,32,128]{5,4,3,2,1,0:T(8,128)S(1)} %pad_maximum_fusion), channel_id=1, source_target_pairs={{0,1},{1,2},{2,3},{3,4},{4,5},{5,6},{6,7},{7,0},{8,9},{9,10},{10,1... | collective-permute-start | bytes 884744 | tf_op jit(solution)/shard_map/ppermute | solution.py:14
  27.8 15.3 %collective-permute-start.4 = (f32[3,3,1,2,32,128]{5,4,3,2,1,0:T(8,128)S(1)}, f32[3,3,1,2,32,128]{5,4,3,2,1,0:T(8,128)S(1)}, u32[]{:S(2)}, u32[]{:S(2)}) collective-permute-start(f32[3,3,1,2,32,128]{5,4,3,2,1,0:T(8,128)S(1)} %pad_maximum_fusion), channel_id=1, source_target_pairs={{1,0},{2,1},{3,2},{4,3},{5,4},{6,5},{7,6},{0,7},{9,8},{10,9},{11,1... | collective-permute-start | bytes 884744 | tf_op jit(solution)/shard_map/ppermute | solution.py:16
  142.3 6.0 collective-permute-start.7
  146.4 7.0 %collective-permute-start.6 = (f32[1,1,1,2,32,128]{5,4,3,2,1,0:T(8,128)S(1)}, f32[1,1,1,2,32,128]{5,4,3,2,1,0:T(8,128)S(1)}, u32[]{:S(2)}, u32[]{:S(2)}) collective-permute-start(f32[1,1,1,2,32,128]{5,4,3,2,1,0:T(8,128)S(1)} %get-tuple-element.9), channel_id=1, source_target_pairs={{64,0},{128,64},{192,128},{256,192},{320,256},{384,320},{448,384},... | collective-permute-start | bytes 98312 | tf_op jit(solution)/shard_map/ppermute | solution.py:16
  153.4 4.1 collective-permute-start.9
  153.4 4.0 collective-permute-start.8
  157.5 207.5 %copy-start.4 = (f32[1,1,1,2,32,128]{5,4,3,2,1,0:T(8,128)S(1)}, f32[1,1,1,2,32,128]{5,4,3,2,1,0:T(8,128)}, u32[]{:S(2)}) copy-start(f32[1,1,1,2,32,128]{5,4,3,2,1,0:T(8,128)} %param.7) | copy-start | bytes 98308
  157.5 207.7 %copy-start.5 = (s32[1,1,1,2]{3,2,1,0:T(1,128)S(1)}, s32[1,1,1,2]{3,2,1,0:T(1,128)}, u32[]{:S(2)}) copy-start(s32[1,1,1,2]{3,2,1,0:T(1,128)} %param.8) | copy-start | bytes 28
  157.5 13.3 %collective-permute-start.11 = (f32[3,3,1,2,32,128]{5,4,3,2,1,0:T(8,128)S(1)}, f32[3,3,1,2,32,128]{5,4,3,2,1,0:T(8,128)S(1)}, u32[]{:S(2)}, u32[]{:S(2)}) collective-permute-start(f32[3,3,1,2,32,128]{5,4,3,2,1,0:T(8,128)S(1)} %pad_maximum_fusion.1), channel_id=1, source_target_pairs={{0,1},{1,2},{2,3},{3,4},{4,5},{5,6},{6,7},{7,0},{8,9},{9,10},{10,1... | collective-permute-start | bytes 884744 | tf_op jit(solution)/shard_map/ppermute | solution.py:14
  159.5 11.4 %collective-permute-start.10 = (f32[3,3,1,2,32,128]{5,4,3,2,1,0:T(8,128)S(1)}, f32[3,3,1,2,32,128]{5,4,3,2,1,0:T(8,128)S(1)}, u32[]{:S(2)}, u32[]{:S(2)}) collective-permute-start(f32[3,3,1,2,32,128]{5,4,3,2,1,0:T(8,128)S(1)} %pad_maximum_fusion.1), channel_id=1, source_target_pairs={{1,0},{2,1},{3,2},{4,3},{5,4},{6,5},{7,6},{0,7},{9,8},{10,9},{11,1... | collective-permute-start | bytes 884744 | tf_op jit(solution)/shard_map/ppermute | solution.py:16
  365.0 4.2 copy-start.3
Sparse Core Ops, SparseCore 0:
  369.4 267.7 all-reduce.3
where the time goes:
time: 680 us; the launch traced here: 679 us
  blocking collectives  317 us (47%)
  waiting for transfers between devices  294 us (43%)
  starting transfers between devices  36.3 us (5%)
  between operations  14.3 us (2%)
  matrix products  10.4 us (2%)
  local copies, waits for them, and re-layouts  7.46 us (1%)
    psum x1, waiting for transfers between devices, body(): coarse_rhs = lax.psum(partial_rhs, ('ta', 'gz', 'xy'))  268 us
    psum x1, blocking collectives, body(): lax.psum(inner_sum(image_first, image_raw), ('ta', 'gz', 'xy'))  97.8 us
    psum x1, blocking collectives, body(): lax.psum((inner_sum(image_first, right_side), inner_sum(image_first, imag...  97.5 us
    psum x1, blocking collectives, body(): lax.psum((inner_sum(image_second, resid_mid), inner_sum(image_second, ima...  94.5 us
    all_gather x1, blocking collectives, body(): correction = lax.all_gather(rows_part, 'xy', axis=0, tiled=True)  26.9 us
    ppermute x6, starting transfers between devices, extended(): lax.ppermute(head, axis, [((i + 1) % count, i) for i in range(count)])  21 us
    ppermute x6, waiting for transfers between devices, extended(): lax.ppermute(head, axis, [((i + 1) % count, i) for i in range(count)])  21 us
    ppermute x6, starting transfers between devices, extended(): lax.ppermute(tail, axis, [(i, (i + 1) % count) for i in range(count)])  15.2 us
  transfers between devices with their start and end apart: 13, of which 7 were waited for; matrix products, arithmetic and copies ran while one was open for 0% of the time, Pallas kernels for 0%

commit v1 on v0

--- a/solution.py
+++ b/solution.py
@@ -56,7 +56,9 @@
     step_first = cross_first / square_first
     resid_mid = right_side - step_first[:, None] * image_first
     image_raw = apply_operator(resid_mid, stencil)
-    correlation_sum = lax.psum(inner_sum(image_first, image_raw), ("ta", "gz", "xy"))
+    x = inner_sum(image_first, image_raw)
+    parts = lax.all_gather(x, ("ta", "gz", "xy"))
+    correlation_sum = jnp.sum(parts, axis=0)
     beta = correlation_sum / square_first
     image_second = image_raw - beta[:, None] * image_first
     direction = resid_mid - beta[:, None] * right_side

time: 680 us -> 845 us (1.24)
  waiting for transfers between devices: 294 us -> 546 us
  blocking collectives: 317 us -> 221 us
    unnamed x1 -> x3, waiting for transfers between devices: 0.02 us -> 257 us
    psum x1 -> x0, blocking collectives: 97.8 us -> none  [body(): lax.psum(inner_sum(image_first, image_raw), ('ta', 'gz', 'xy'))]
  transfers between devices with their start and end apart: 13 -> 14, of which waited for: 7 -> 8; matrix products, arithmetic and copies ran while one was open for 0% -> 1% of each run, Pallas kernels for 0% -> 0%
where the time goes in v1:
time: 845 us; the launch traced here: 844 us
  waiting for transfers between devices  546 us (65%)
  blocking collectives  221 us (26%)
  starting transfers between devices  36.4 us (4%)
  between operations  14.3 us (2%)
  local copies, waits for them, and re-layouts  13.6 us (2%)
  matrix products  11.4 us (1%)
    psum x1, waiting for transfers between devices, body(): coarse_rhs = lax.psum(partial_rhs, ('ta', 'gz', 'xy'))  266 us
    unnamed x3, waiting for transfers between devices  257 us
    psum x1, blocking collectives, body(): lax.psum((inner_sum(image_first, right_side), inner_sum(image_first, imag...  97.5 us
    psum x1, blocking collectives, body(): lax.psum((inner_sum(image_second, resid_mid), inner_sum(image_second, ima...  96.6 us
    all_gather x1, blocking collectives, body(): correction = lax.all_gather(rows_part, 'xy', axis=0, tiled=True)  26.9 us
    ppermute x6, starting transfers between devices, extended(): lax.ppermute(head, axis, [((i + 1) % count, i) for i in range(count)])  21 us
    ppermute x6, waiting for transfers between devices, extended(): lax.ppermute(head, axis, [((i + 1) % count, i) for i in range(count)])  19.2 us
  transfers between devices with their start and end apart: 14, of which 8 were waited for; matrix products, arithmetic and copies ran while one was open for 1% of the time, Pallas kernels for 0%

profile of v1, /device:TPU:26, one launch (start us, length us, event | category | flops | bytes accessed | tf_op | source)
XLA Modules:
  0.0 844.1 jit_solution(17492289732740257554)
XLA Ops:
  7.2 5.0 collective-permute-start.1
  12.2 1.9 collective-permute-start
  17.0 2.4 collective-permute-done
  19.5 1.7 collective-permute-start.2
  23.5 4.3 collective-permute-start.5
  27.8 8.6 %collective-permute-start.4 = (f32[3,3,1,2,32,128]{5,4,3,2,1,0:T(8,128)S(1)}, f32[3,3,1,2,32,128]{5,4,3,2,1,0:T(8,128)S(1)}, u32[]{:S(2)}, u32[]{:S(2)}) collective-permute-start(f32[3,3,1,2,32,128]{5,4,3,2,1,0:T(8,128)S(1)} %pad_maximum_fusion), channel_id=1, source_target_pairs={{1,0},{2,1},{3,2},{4,3},{5,4},{6,5},{7,6},{0,7},{9,8},{10,9},{11,1... | collective-permute-start | bytes 884744 | tf_op jit(solution)/shard_map/ppermute | solution.py:16
  37.6 5.5 collective-permute-done.4
  45.6 2.4 fusion.6
  48.1 97.5 %all-reduce.2 = (f32[32]{0:T(128)S(1)}, f32[32]{0:T(128)S(1)}) all-reduce(f32[32]{0:T(128)S(1)} %get-tuple-element.14, f32[32]{0:T(128)S(1)} %fusion.13), channel_id=1, replica_groups=mesh['ta'=8,'gz'=8,'xy'=8] {'ta','gz','xy'}, use_global_device_ids=true, to_apply=%region_1.2 | all-reduce | flops 64 | bytes 512 | tf_op jit(solution)/shard_map/psum | solution.py:52
  145.7 4.1 collective-permute-start.7
  149.7 1.9 collective-permute-start.6
  151.7 5.1 collective-permute-done.6
  156.8 1.7 collective-permute-start.8
  158.5 2.3 collective-permute-done.9
  160.9 1.9 collective-permute-start.11
  162.8 5.1 collective-permute-start.10
  167.9 6.2 collective-permute-done.10
  176.6 256.7 %all-reduce.8.cloned.1.call-done = f32[16384]{0:T(1024)} async-done(((f32[16384]{0:T(1024)}), f32[16384]{0:T(1024)}) %all-reduce.8.cloned.1.call-update) | async-done | bytes 65552
  434.7 96.6 %all-reduce.1 = (f32[32]{0:T(128)S(1)}, f32[32]{0:T(128)S(1)}) all-reduce(f32[32]{0:T(128)S(1)} %fusion.11, f32[32]{0:T(128)S(1)} %get-tuple-element.6), channel_id=1, replica_groups=mesh['ta'=8,'gz'=8,'xy'=8] {'ta','gz','xy'}, use_global_device_ids=true, to_apply=%region_7.8 | all-reduce | flops 64 | bytes 512 | tf_op jit(solution)/shard_map/psum | solution.py:65
  531.6 1.4 convolution_bitcast_fusion
  535.6 266.4 %all-reduce.6.cloned.1.call-done = f32[2048,32]{0,1:T(8,128)} async-done(((f32[2048,32]{0,1:T(8,128)}), f32[2048,32]{0,1:T(8,128)}) %all-reduce.6.cloned.1.call-update) | async-done | bytes 262160 | tf_op jit(solution)/shard_map/psum | solution.py:85
  802.0 2.9 convolution_bitcast_fusion.2
  804.9 26.9 %all_gather.11 = f32[2048,32]{0,1:T(8,128)} all-gather(f32[256,32]{0,1:T(8,128)S(1)} %convolution_bitcast_fusion.2), channel_id=1, replica_groups=mesh['ta'=8,'gz'=8,'xy'=8] {'xy'}, dimensions={0}, use_global_device_ids=true | all-gather | bytes 294912 | tf_op jit(solution)/shard_map/all_gather | solution.py:92
  834.3 2.2 fusion.17
  (71 shorter events, 19.2 us)
Async XLA Ops:
  7.2 794.8 %copy-start = (f32[256,2048]{1,0:T(8,128)S(1)}, f32[256,2048]{1,0:T(8,128)}, u32[]{:S(2)}) copy-start(f32[256,2048]{1,0:T(8,128)} %param.9) | copy-start | bytes 6291460
  7.2 38.4 %copy-start.2 = (f32[1,1,1,2,32,128]{5,4,3,2,1,0:T(8,128)S(1)}, f32[1,1,1,2,32,128]{5,4,3,2,1,0:T(8,128)}, u32[]{:S(2)}) copy-start(f32[1,1,1,2,32,128]{5,4,3,2,1,0:T(8,128)} %param.5) | copy-start | bytes 98308
  7.2 38.4 %copy-start.1 = (f32[1,1,1,2,9,128,128]{6,5,4,3,2,1,0:T(8,128)S(1)}, f32[1,1,1,2,9,128,128]{6,5,4,3,2,1,0:T(8,128)}, u32[]{:S(2)}) copy-start(f32[1,1,1,2,9,128,128]{6,5,4,3,2,1,0:T(8,128)} %param.6) | copy-start | bytes 3538948
  7.2 426.2 %all-reduce.8.cloned.1.call-start = ((), (), s32[]{:S(2)}) async-start(), calls=%async_computation.1 | async-start | bytes 131072
  7.2 9.0 %collective-permute-start.1 = (f32[1,1,1,2,32,128]{5,4,3,2,1,0:T(8,128)}, f32[1,1,1,2,32,128]{5,4,3,2,1,0:T(8,128)S(1)}, u32[]{:S(2)}, u32[]{:S(2)}) collective-permute-start(f32[1,1,1,2,32,128]{5,4,3,2,1,0:T(8,128)} %param.5), channel_id=1, source_target_pairs={{0,64},{64,128},{128,192},{192,256},{256,320},{320,384},{384,448},... | collective-permute-start | bytes 98312 | tf_op jit(solution)/shard_map/ppermute | solution.py:14
  12.2 7.2 collective-permute-start
  19.5 4.0 collective-permute-start.3
  19.5 4.0 collective-permute-start.2
  23.5 20.2 %collective-permute-start.5 = (f32[3,3,1,2,32,128]{5,4,3,2,1,0:T(8,128)S(1)}, f32[3,3,1,2,32,128]{5,4,3,2,1,0:T(8,128)S(1)}, u32[]{:S(2)}, u32[]{:S(2)}) collective-permute-start(f32[3,3,1,2,32,128]{5,4,3,2,1,0:T(8,128)S(1)} %pad_maximum_fusion), channel_id=1, source_target_pairs={{0,1},{1,2},{2,3},{3,4},{4,5},{5,6},{6,7},{7,0},{8,9},{9,10},{10,1... | collective-permute-start | bytes 884744 | tf_op jit(solution)/shard_map/ppermute | solution.py:14
  27.8 15.3 %collective-permute-start.4 = (f32[3,3,1,2,32,128]{5,4,3,2,1,0:T(8,128)S(1)}, f32[3,3,1,2,32,128]{5,4,3,2,1,0:T(8,128)S(1)}, u32[]{:S(2)}, u32[]{:S(2)}) collective-permute-start(f32[3,3,1,2,32,128]{5,4,3,2,1,0:T(8,128)S(1)} %pad_maximum_fusion), channel_id=1, source_target_pairs={{1,0},{2,1},{3,2},{4,3},{5,4},{6,5},{7,6},{0,7},{9,8},{10,9},{11,1... | collective-permute-start | bytes 884744 | tf_op jit(solution)/shard_map/ppermute | solution.py:16
  145.7 6.0 collective-permute-start.7
  149.7 7.0 collective-permute-start.6
  156.8 4.1 collective-permute-start.9
  156.8 4.0 collective-permute-start.8
  160.9 13.3 %collective-permute-start.11 = (f32[3,3,1,2,32,128]{5,4,3,2,1,0:T(8,128)S(1)}, f32[3,3,1,2,32,128]{5,4,3,2,1,0:T(8,128)S(1)}, u32[]{:S(2)}, u32[]{:S(2)}) collective-permute-start(f32[3,3,1,2,32,128]{5,4,3,2,1,0:T(8,128)S(1)} %pad_maximum_fusion.1), channel_id=1, source_target_pairs={{0,1},{1,2},{2,3},{3,4},{4,5},{5,6},{6,7},{7,0},{8,9},{9,10},{10,1... | collective-permute-start | bytes 884744 | tf_op jit(solution)/shard_map/ppermute | solution.py:14
  162.8 11.4 %collective-permute-start.10 = (f32[3,3,1,2,32,128]{5,4,3,2,1,0:T(8,128)S(1)}, f32[3,3,1,2,32,128]{5,4,3,2,1,0:T(8,128)S(1)}, u32[]{:S(2)}, u32[]{:S(2)}) collective-permute-start(f32[3,3,1,2,32,128]{5,4,3,2,1,0:T(8,128)S(1)} %pad_maximum_fusion.1), channel_id=1, source_target_pairs={{1,0},{2,1},{3,2},{4,3},{5,4},{6,5},{7,6},{0,7},{9,8},{10,9},{11,1... | collective-permute-start | bytes 884744 | tf_op jit(solution)/shard_map/ppermute | solution.py:16
  174.2 357.2 %copy-start.5 = (f32[1,1,1,2,32,128]{5,4,3,2,1,0:T(8,128)S(1)}, f32[1,1,1,2,32,128]{5,4,3,2,1,0:T(8,128)}, u32[]{:S(2)}) copy-start(f32[1,1,1,2,32,128]{5,4,3,2,1,0:T(8,128)} %param.7) | copy-start | bytes 98308
  174.2 357.3 %copy-start.6 = (s32[1,1,1,2]{3,2,1,0:T(1,128)S(1)}, s32[1,1,1,2]{3,2,1,0:T(1,128)}, u32[]{:S(2)}) copy-start(s32[1,1,1,2]{3,2,1,0:T(1,128)} %param.8) | copy-start | bytes 28
  176.0 0.6 copy-start.3
  176.6 625.4 %all-reduce.6.cloned.1.call-start = ((), (), s32[]{:S(2)}) async-start(), calls=%async_computation | async-start | bytes 524288 | tf_op jit(solution)/shard_map/psum | solution.py:85
  531.4 4.2 copy-start.4
Sparse Core Ops, SparseCore 0:
  176.7 256.6 all-reduce.7
  535.7 266.2 all-reduce.5
